TPU v7x, 32 devices: a whole 2x2x4 slice. The times are simulated.
32 devices in a mesh: grp: 2 (over x), area: 8 (over z, y), ctg: 2 (over core).
Axes of the slice: x: 2, y: 2, z: 4, core: 2. Of those that a mesh axis runs over, the one named last changes fastest.
Arguments:
- area_size: int32 [16], P(('grp', 'area')), parts along dimension 0, may hold values from 299 to 1024, as said below
- tie_peer: int32 [16, 42], P(('grp', 'area')), parts along dimension 0, may hold values from 0 to 7, as said below
- kkt_diag: float32 [16, 2, 1024], P(('grp', 'area'), 'ctg'), parts along dimension 0, may hold values from 0.5 to 1
- kkt_offdiag: float32 [16, 2, 1024, 1024], P(('grp', 'area'), 'ctg'), parts along dimension 0, may hold values from -0.1875 to 0.1875
- cost: float32 [16, 2, 1024, 256], P(('grp', 'area'), 'ctg'), parts along dimension 0, may hold values from -6 to 6
- consensus: float32 [16, 2, 1024, 256], P(('grp', 'area'), 'ctg'), parts along dimension 0, may hold values from -4 to 4
- dual: float32 [16, 2, 1024, 256], P(('grp', 'area'), 'ctg'), parts along dimension 0, may hold values from -4 to 4
- limit: float32 [16, 1024, 256], P(('grp', 'area')), parts along dimension 0, may hold values from 0.3 to 1.5
Outputs:
- agreed_out: float32 [16, 2, 1024, 256], P(('grp', 'area'), 'ctg'), parts along dimension 0
- dual_out: float32 [16, 2, 1024, 256], P(('grp', 'area'), 'ctg'), parts along dimension 0
There are 2 independent parts, one for each index of `grp`. A program takes and returns all parts, laid end to end along the dimension named above; each array names one. Nothing has to cross between parts.
Inputs may be any that keep to these rules, and one draw needn't show every extreme that they name: `area_size`: some area has exactly 1024 live slots. `tie_peer`: never the area itself; each area has exactly 6 tie slots to each other area.
All inputs are finite; a program needn't handle non-finite values.
Results may differ from a plain program's by a relative error of at most 0.0003.
Values sent between devices are 32-bit elements; how exact they have to be, the bound alone decides.
No kernel may reach another device: no remote copies, remote signals or barrier semaphores. Data moves between devices by JAX's collectives and lax.ppermute only.
A program may use at most 64 MiB of HBM per device.

v0:
```python
import jax
import jax.numpy as jnp
from jax import lax
from jax.sharding import PartitionSpec as P

GENS = 256
ITERS = 3


def tie_dest(peers, pair_lines):
    count = peers.shape[0]
    order = jnp.arange(count)
    same = (peers[:, None] == peers[None, :]) & (order[:, None] < order[None, :])
    rank = jnp.sum(same.astype(jnp.int32), axis=0)
    return peers * pair_lines + rank


def apply_rows(matrix, right_side):
    return jnp.dot(
        matrix, right_side, precision=lax.Precision.HIGHEST, preferred_element_type=jnp.float32
    )


def local(area_size, tie_peer, kkt_diag, kkt_offdiag, cost, consensus, dual, limit):
    areas = lax.axis_size("area")
    scenarios = lax.axis_size("ctg")
    peers = tie_peer[0]
    ties = peers.shape[0]
    pair_lines = ties // (areas - 1)
    dest = tie_dest(peers, pair_lines)
    slots = cost.shape[2]
    hours = cost.shape[3]
    shared = GENS + ties
    live = (jnp.arange(slots) < area_size[0]).astype(jnp.float32)[:, None]
    offdiag = kkt_offdiag[0, 0]
    diagonal = kkt_diag[0, 0][:, None]
    bound = limit[0]
    linear = cost[0, 0]
    agreed = consensus[0, 0]
    dual_var = dual[0, 0]
    for iteration in range(ITERS):
        right_side = live * (agreed - dual_var - linear)
        primal = live * (diagonal * right_side + apply_rows(offdiag, right_side))
        primal_top = primal[:shared]
        dual_top = dual_var[:shared]
        shifted = primal_top + dual_top
        gen_mean = lax.psum(shifted[:GENS], "ctg") / scenarios
        empty = jnp.zeros((areas * pair_lines, hours), jnp.float32)
        sent_primal = empty.at[dest].set(primal_top[GENS:])
        sent_dual = empty.at[dest].set(dual_top[GENS:])
        got_primal = lax.all_to_all(sent_primal, "area", split_axis=0, concat_axis=0, tiled=True)
        got_dual = lax.all_to_all(sent_dual, "area", split_axis=0, concat_axis=0, tiled=True)
        other = got_primal[dest] + got_dual[dest]
        top_part = jnp.concatenate([gen_mean, 0.5 * (shifted[GENS:] + other)], axis=0)
        averaged = jnp.concatenate([top_part, primal[shared:] + dual_var[shared:]], axis=0)
        agreed = live * jnp.clip(averaged, -bound, bound)
        dual_var = live * (dual_var + primal - agreed)
    return (agreed[None, None], dual_var[None, None])


def solution(mesh):
    return jax.shard_map(
        local,
        mesh=mesh,
        in_specs=(
            P(("grp", "area")),
            P(("grp", "area"), None),
            P(("grp", "area"), "ctg", None),
            P(("grp", "area"), "ctg", None, None),
            P(("grp", "area"), "ctg", None, None),
            P(("grp", "area"), "ctg", None, None),
            P(("grp", "area"), "ctg", None, None),
            P(("grp", "area"), None, None),
        ),
        out_specs=(P(("grp", "area"), "ctg", None, None), P(("grp", "area"), "ctg", None, None)),
        check_vma=False,
    )
```

profile of v0, /device:TPU:0, one launch (start us, length us, event | category | flops | bytes accessed | tf_op | source)
XLA Modules:
  0.0 138.7 jit_solution(8805056950843362891)
XLA Ops:
  7.2 0.8 convert_reduce_fusion
  8.0 0.7 fusion.85
  8.6 1.0 scatter_custom_fusion.1
  9.7 0.6 all_to_all.51
  10.3 7.3 %all-to-all-start.1 = ((f32[8,6,256]{2,1,0:T(8,128)}), f32[8,6,256]{2,1,0:T(8,128)S(1)}, u32[]{:S(2)}, u32[]{:S(2)}) async-start(f32[8,6,256]{2,1,0:T(8,128)} %all_to_all.51), calls=%async_computation.1 | async-start | bytes 131072 | tf_op jit(solution)/shard_map/all_to_all | solution.py:52
  17.6 0.0 all-reduce.4.cloned.1.call-start
  18.3 0.0 copy-start.4
  18.3 7.7 %fusion.12 = f32[1024,256]{1,0:T(8,128)S(1)} fusion(f32[1,1,1024,1024]{3,2,1,0:T(8,128)} %param.11, f32[1,1,1024,256]{3,2,1,0:T(8,128)} %param.12, f32[1,1,1024,256]{3,2,1,0:T(8,128)} %param.14, f32[1,1,1024,256]{3,2,1,0:T(8,128)} %param.13, f32[1024]{0:T(1024)} %bitcast.144, f32[1024]{0:T(1024)S(1)} %fusion.84), kind=kOutput, calls=%fused_computation.20 | convolution fusion | flops 3223584768 | bytes 8396800 | tf_op jit(solution)/shard_map/dot_general | solution.py:19
  26.0 0.0 copy-start.5
  26.0 1.0 copy-done.5
  27.0 0.7 slice.127
  27.8 0.0 all-reduce.4.cloned.1.call-update
  27.8 1.3 slice_add_fusion.2
  29.1 0.0 copy-start.7
  29.1 1.0 scatter_custom_fusion
  30.1 0.6 all_to_all.48
  30.8 6.0 %all-to-all-start = ((f32[8,6,256]{2,1,0:T(8,128)}), f32[8,6,256]{2,1,0:T(8,128)S(1)}, u32[]{:S(2)}, u32[]{:S(2)}) async-start(f32[8,6,256]{2,1,0:T(8,128)} %all_to_all.48), calls=%async_computation | async-start | bytes 131072 | tf_op jit(solution)/shard_map/all_to_all | solution.py:51
  36.7 0.6 gather_fusion.1
  37.4 6.3 %all-to-all-done = f32[8,6,256]{2,1,0:T(8,128)S(1)} async-done(((f32[8,6,256]{2,1,0:T(8,128)}), f32[8,6,256]{2,1,0:T(8,128)S(1)}, u32[]{:S(2)}, u32[]{:S(2)}) %all-to-all-start) | async-done | bytes 49184 | tf_op jit(solution)/shard_map/all_to_all | solution.py:51
  43.6 0.6 gather_fusion
  44.3 3.3 %all-reduce.4.cloned.1.call-done = f32[256,256]{1,0:T(8,128)} async-done(((f32[256,256]{1,0:T(8,128)}), f32[256,256]{1,0:T(8,128)}) %all-reduce.4.cloned.1.call-update) | async-done | bytes 262160 | tf_op jit(solution)/shard_map/psum | solution.py:47
  47.5 1.1 broadcast_multiply_fusion.2
  48.7 2.1 %fusion.50 = f32[1024,256]{1,0:T(8,128)S(1)} fusion(f32[1024,256]{1,0:T(8,128)} %copy-done.5, f32[1,1,1024,256]{3,2,1,0:T(8,128)} %param.14, f32[1024]{0:T(1024)S(1)} %fusion.84, f32[726,256]{1,0:T(8,128)S(1)} %slice_add_fusion.2, f32[42,256]{1,0:T(8,128)S(1)} %fusion.73, f32[256,256]{1,0:T(8,128)S(1)} %broadcast_multiply_fusion.2, ...), kind=kLoop, calls=%fused_computation.53 | loop fusion | flops 2359296 | bytes 5246976 | tf_op jit(solution)/shard_map/mul | solution.py:57
  50.8 6.5 %fusion.21 = f32[1024,256]{1,0:T(8,128)} fusion(f32[1,1,1024,1024]{3,2,1,0:T(8,128)S(1)} %copy-done, f32[1,1,1024,256]{3,2,1,0:T(8,128)} %param.12, f32[1024,256]{1,0:T(8,128)S(1)} %fusion.50, f32[1024]{0:T(1024)S(1)} %bitcast.145, f32[1024]{0:T(1024)S(1)} %fusion.84, f32[726,256]{1,0:T(8,128)S(1)} %slice_add_fusion.2, f32[42,256]{1,0:T(8,128)S(1)} %fusion.73, ...), kind=kOutput, calls=%fused_computation.23 | convolution fusion | flops 3226730496 | bytes 9445376 | tf_op jit(solution)/shard_map/dot_general | solution.py:19
  57.4 1.0 scatter_custom_fusion.2
  58.4 0.6 all_to_all.54
  59.0 5.8 %all-to-all-start.2 = ((f32[8,6,256]{2,1,0:T(8,128)}), f32[8,6,256]{2,1,0:T(8,128)S(1)}, u32[]{:S(2)}, u32[]{:S(2)}) async-start(f32[8,6,256]{2,1,0:T(8,128)} %all_to_all.54), calls=%async_computation.2 | async-start | bytes 131072 | tf_op jit(solution)/shard_map/all_to_all | solution.py:51
  64.8 0.0 all-reduce.6.cloned.1.call-start
  64.9 1.0 slice_add_fusion.4
  65.9 0.7 scatter_custom_fusion.3
  66.6 0.6 all_to_all.57
  67.3 0.7 slice.133
  68.0 0.0 all-reduce.6.cloned.1.call-update
  68.0 3.7 %all-to-all-done.2 = f32[8,6,256]{2,1,0:T(8,128)S(1)} async-done(((f32[8,6,256]{2,1,0:T(8,128)}), f32[8,6,256]{2,1,0:T(8,128)S(1)}, u32[]{:S(2)}, u32[]{:S(2)}) %all-to-all-start.2) | async-done | bytes 49184 | tf_op jit(solution)/shard_map/all_to_all | solution.py:51
  71.8 3.5 %all-to-all-start.3 = ((f32[8,6,256]{2,1,0:T(8,128)}), f32[8,6,256]{2,1,0:T(8,128)S(1)}, u32[]{:S(2)}, u32[]{:S(2)}) async-start(f32[8,6,256]{2,1,0:T(8,128)} %all_to_all.57), calls=%async_computation.3 | async-start | bytes 131072 | tf_op jit(solution)/shard_map/all_to_all | solution.py:52
  75.3 2.1 %slice_add_fusion.1 = f32[726,256]{1,0:T(8,128)} fusion(f32[1024,256]{1,0:T(8,128)S(1)} %fusion.50, f32[1024,256]{1,0:T(8,128)} %fusion.21), kind=kLoop, calls=%fused_computation.63 | loop fusion | flops 185856 | bytes 2230272 | tf_op jit(solution)/shard_map/add | solution.py:55
  77.4 0.6 gather_fusion.2
  78.0 3.9 %all-to-all-done.3 = f32[8,6,256]{2,1,0:T(8,128)S(1)} async-done(((f32[8,6,256]{2,1,0:T(8,128)}), f32[8,6,256]{2,1,0:T(8,128)S(1)}, u32[]{:S(2)}, u32[]{:S(2)}) %all-to-all-start.3) | async-done | bytes 49184 | tf_op jit(solution)/shard_map/all_to_all | solution.py:52
  82.0 0.6 gather_fusion.3
  82.6 5.1 %all-reduce.6.cloned.1.call-done = f32[256,256]{1,0:T(8,128)} async-done(((f32[256,256]{1,0:T(8,128)}), f32[256,256]{1,0:T(8,128)}) %all-reduce.6.cloned.1.call-update) | async-done | bytes 262160 | tf_op jit(solution)/shard_map/psum | solution.py:47
  87.7 1.1 broadcast_multiply_fusion.1
  88.9 2.3 %subtract_multiply_fusion = f32[1024,256]{1,0:T(8,128)S(1)} fusion(f32[1024,256]{1,0:T(8,128)S(1)} %fusion.50, f32[1024,256]{1,0:T(8,128)} %fusion.21, f32[1024]{0:T(1024)S(1)} %fusion.84, f32[726,256]{1,0:T(8,128)} %slice_add_fusion.1, f32[42,256]{1,0:T(8,128)S(1)} %fusion.70, f32[256,256]{1,0:T(8,128)S(1)} %broadcast_multiply_fusion.1, ...), kind=kLoop, calls=%fused_computation.57 | loop fusion | flops 2359296 | bytes 5246976 | tf_op jit(solution)/shard_map/mul | solution.py:57
  91.2 5.6 %fusion.30 = f32[1024,256]{1,0:T(8,128)S(1)} fusion(f32[1,1,1024,1024]{3,2,1,0:T(8,128)S(1)} %copy-done.1, f32[1,1,1024,256]{3,2,1,0:T(8,128)} %param.12, f32[1024,256]{1,0:T(8,128)S(1)} %subtract_multiply_fusion, f32[1024]{0:T(1024)S(1)} %bitcast.146, f32[1024]{0:T(1024)S(1)} %fusion.84, f32[726,256]{1,0:T(8,128)S(1)} %copy-done.3, ...), kind=kOutput, calls=%fused_computation.26 | convolution fusion | flops 3226730496 | bytes 9445376 | tf_op jit(solution)/shard_map/dot_general | solution.py:19
  96.8 0.7 scatter_custom_fusion.4
  97.5 0.6 all_to_all.60
  98.2 5.8 %all-to-all-start.4 = ((f32[8,6,256]{2,1,0:T(8,128)}), f32[8,6,256]{2,1,0:T(8,128)}, u32[]{:S(2)}, u32[]{:S(2)}) async-start(f32[8,6,256]{2,1,0:T(8,128)} %all_to_all.60), calls=%async_computation.4 | async-start | bytes 131072 | tf_op jit(solution)/shard_map/all_to_all | solution.py:51
  104.0 0.0 all-reduce.8.cloned.1.call-start
  104.1 0.7 scatter_custom_fusion.5
  104.8 0.6 all_to_all.63
  105.5 0.7 slice.141
  106.2 0.0 all-reduce.8.cloned.1.call-update
  106.2 4.8 %all-to-all-done.4 = f32[8,6,256]{2,1,0:T(8,128)} async-done(((f32[8,6,256]{2,1,0:T(8,128)}), f32[8,6,256]{2,1,0:T(8,128)}, u32[]{:S(2)}, u32[]{:S(2)}) %all-to-all-start.4) | async-done | bytes 49184 | tf_op jit(solution)/shard_map/all_to_all | solution.py:51
  111.0 4.0 %all-to-all-start.5 = ((f32[8,6,256]{2,1,0:T(8,128)}), f32[8,6,256]{2,1,0:T(8,128)}, u32[]{:S(2)}, u32[]{:S(2)}) async-start(f32[8,6,256]{2,1,0:T(8,128)} %all_to_all.63), calls=%async_computation.5 | async-start | bytes 131072 | tf_op jit(solution)/shard_map/all_to_all | solution.py:52
  115.0 1.0 slice_add_fusion
  116.0 0.8 all_to_all.62
  116.8 1.2 gather_fusion.4
  118.0 3.9 %all-to-all-done.5 = f32[8,6,256]{2,1,0:T(8,128)} async-done(((f32[8,6,256]{2,1,0:T(8,128)}), f32[8,6,256]{2,1,0:T(8,128)}, u32[]{:S(2)}, u32[]{:S(2)}) %all-to-all-start.5) | async-done | bytes 49184 | tf_op jit(solution)/shard_map/all_to_all | solution.py:52
  121.9 0.8 all_to_all.65
  122.7 1.2 gather_fusion.5
  124.0 0.8 fusion.65
  124.8 2.5 %all-reduce.8.cloned.1.call-done = f32[256,256]{1,0:T(8,128)} async-done(((f32[256,256]{1,0:T(8,128)}), f32[256,256]{1,0:T(8,128)}) %all-reduce.8.cloned.1.call-update) | async-done | bytes 262160 | tf_op jit(solution)/shard_map/psum | solution.py:47
  127.3 1.1 broadcast_multiply_fusion
  128.4 2.5 %fusion.43 = f32[1,1,1024,256]{3,2,1,0:T(8,128)} fusion(f32[726,256]{1,0:T(8,128)} %slice_add_fusion, f32[42,256]{1,0:T(8,128)S(1)} %fusion.65, f32[256,256]{1,0:T(8,128)S(1)} %get-tuple-element.8, f32[1,1024,256]{2,1,0:T(8,128)S(1)} %copy-done.2, f32[1024,256]{1,0:T(8,128)S(1)} %subtract_multiply_fusion, f32[1024,256]{1,0:T(8,128)S(1)} %fusion.30, ...), kind=kLoop, calls=%fused_computation.41 | loop fusion | flops 2359296 | bytes 5246976 | tf_op jit(solution)/shard_map/broadcast_in_dim | solution.py:58
  130.9 1.3 fusion.38
  (23 shorter events, 0.2 us)
Async XLA Ops:
  10.3 20.5 %all-to-all-start.1 = ((f32[8,6,256]{2,1,0:T(8,128)}), f32[8,6,256]{2,1,0:T(8,128)S(1)}, u32[]{:S(2)}, u32[]{:S(2)}) async-start(f32[8,6,256]{2,1,0:T(8,128)} %all_to_all.51), calls=%async_computation.1 | async-start | bytes 131072 | tf_op jit(solution)/shard_map/all_to_all | solution.py:52
  17.6 29.9 %all-reduce.4.cloned.1.call-start = ((), (), s32[]{:S(2)}) async-start(), calls=%async_computation.6 | async-start | bytes 524288 | tf_op jit(solution)/shard_map/psum | solution.py:47
  18.3 8.7 %copy-start.4 = (f32[1,1,1024,256]{3,2,1,0:T(8,128)S(1)}, f32[1,1,1024,256]{3,2,1,0:T(8,128)}, u32[]{:S(2)}) copy-start(f32[1,1,1024,256]{3,2,1,0:T(8,128)} %param.14) | copy-start | bytes 3145732
  26.0 1.0 copy-start.5
  27.0 21.7 %copy-start.2 = (f32[1,1024,256]{2,1,0:T(8,128)S(1)}, f32[1,1024,256]{2,1,0:T(8,128)}, u32[]{:S(2)}) copy-start(f32[1,1024,256]{2,1,0:T(8,128)} %param.15) | copy-start | bytes 3145732
  29.1 21.7 %copy-start.7 = (f32[1,1,1024]{2,1,0:T(1,128)S(1)}, f32[1,1,1024]{2,1,0:T(1,128)}, u32[]{:S(2)}) copy-start(f32[1,1,1024]{2,1,0:T(1,128)} %param.10) | copy-start | bytes 12292
  30.8 12.9 %all-to-all-start = ((f32[8,6,256]{2,1,0:T(8,128)}), f32[8,6,256]{2,1,0:T(8,128)S(1)}, u32[]{:S(2)}, u32[]{:S(2)}) async-start(f32[8,6,256]{2,1,0:T(8,128)} %all_to_all.48), calls=%async_computation | async-start | bytes 131072 | tf_op jit(solution)/shard_map/all_to_all | solution.py:51
  47.5 3.3 %copy-start = (f32[1,1,1024,1024]{3,2,1,0:T(8,128)S(1)}, f32[1,1,1024,1024]{3,2,1,0:T(8,128)}, u32[]{:S(2)}) copy-start(f32[1,1,1024,1024]{3,2,1,0:T(8,128)} %param.11) | copy-start | bytes 12582916
  59.0 12.7 %all-to-all-start.2 = ((f32[8,6,256]{2,1,0:T(8,128)}), f32[8,6,256]{2,1,0:T(8,128)S(1)}, u32[]{:S(2)}, u32[]{:S(2)}) async-start(f32[8,6,256]{2,1,0:T(8,128)} %all_to_all.54), calls=%async_computation.2 | async-start | bytes 131072 | tf_op jit(solution)/shard_map/all_to_all | solution.py:51
  64.8 22.9 %all-reduce.6.cloned.1.call-start = ((), (), s32[]{:S(2)}) async-start(), calls=%async_computation.7 | async-start | bytes 524288 | tf_op jit(solution)/shard_map/psum | solution.py:47
  71.8 10.2 %all-to-all-start.3 = ((f32[8,6,256]{2,1,0:T(8,128)}), f32[8,6,256]{2,1,0:T(8,128)S(1)}, u32[]{:S(2)}, u32[]{:S(2)}) async-start(f32[8,6,256]{2,1,0:T(8,128)} %all_to_all.57), calls=%async_computation.3 | async-start | bytes 131072 | tf_op jit(solution)/shard_map/all_to_all | solution.py:52
  87.7 3.4 %copy-start.1 = (f32[1,1,1024,1024]{3,2,1,0:T(8,128)S(1)}, f32[1,1,1024,1024]{3,2,1,0:T(8,128)}, u32[]{:S(2)}) copy-start(f32[1,1,1024,1024]{3,2,1,0:T(8,128)} %param.11) | copy-start | bytes 12582916
  87.7 3.4 %copy-start.3 = (f32[726,256]{1,0:T(8,128)S(1)}, f32[726,256]{1,0:T(8,128)}, u32[]{:S(2)}) copy-start(f32[726,256]{1,0:T(8,128)} %slice_add_fusion.1) | copy-start | bytes 2230276
  98.2 12.8 %all-to-all-start.4 = ((f32[8,6,256]{2,1,0:T(8,128)}), f32[8,6,256]{2,1,0:T(8,128)}, u32[]{:S(2)}, u32[]{:S(2)}) async-start(f32[8,6,256]{2,1,0:T(8,128)} %all_to_all.60), calls=%async_computation.4 | async-start | bytes 131072 | tf_op jit(solution)/shard_map/all_to_all | solution.py:51
  104.0 23.3 %all-reduce.8.cloned.1.call-start = ((), (), s32[]{:S(2)}) async-start(), calls=%async_computation.8 | async-start | bytes 524288 | tf_op jit(solution)/shard_map/psum | solution.py:47
  111.0 10.9 %all-to-all-start.5 = ((f32[8,6,256]{2,1,0:T(8,128)}), f32[8,6,256]{2,1,0:T(8,128)}, u32[]{:S(2)}, u32[]{:S(2)}) async-start(f32[8,6,256]{2,1,0:T(8,128)} %all_to_all.63), calls=%async_computation.5 | async-start | bytes 131072 | tf_op jit(solution)/shard_map/all_to_all | solution.py:52
  127.3 3.5 %copy-start.6 = (f32[726,256]{1,0:T(8,128)S(1)}, f32[726,256]{1,0:T(8,128)}, u32[]{:S(2)}) copy-start(f32[726,256]{1,0:T(8,128)} %slice_add_fusion) | copy-start | bytes 2230276
Sparse Core Ops, SparseCore 0:
  27.9 19.5 all-reduce.3
  68.1 19.5 all-reduce.5
  107.7 19.5 all-reduce.7
where the time goes:
time: 140 us; the launch traced here: 139 us
  waiting for transfers between devices  33.6 us (24%)
  starting transfers between devices  32.5 us (23%)
  matrix products  19.9 us (14%)
  other arithmetic  19.3 us (14%)
  local copies, waits for them, and re-layouts  18.8 us (13%)
  between operations  14.6 us (10%)
    dot_general x3, matrix products, apply_rows(): jnp.dot(matrix, right_side, precision=lax.Precision.HIGHEST, preferred_el...  19.9 us
    all_to_all x3, starting transfers between devices, local(): lax.all_to_all(sent_primal, 'area', split_axis=0, concat_axis=0, tiled=True)  17.6 us
    all_to_all x3, starting transfers between devices, local(): lax.all_to_all(sent_dual, 'area', split_axis=0, concat_axis=0, tiled=True)  14.8 us
    all_to_all x3, waiting for transfers between devices, local(): lax.all_to_all(sent_primal, 'area', split_axis=0, concat_axis=0, tiled=True)  14.8 us
    psum x3, waiting for transfers between devices, local(): gen_mean = lax.psum(shifted[:GENS], 'ctg') / scenarios  10.9 us
    all_to_all x3, waiting for transfers between devices, local(): lax.all_to_all(sent_dual, 'area', split_axis=0, concat_axis=0, tiled=True)  7.78 us
    gather x6, local copies, waits for them, and re-layouts, local(): other = got_primal[dest] + got_dual[dest]  4.91 us
    mul x2, other arithmetic, local(): dual_var = live * (dual_var + primal - agreed)  4.41 us
  transfers between devices with their start and end apart: 9, of which 8 were waited for; matrix products, arithmetic and copies ran while one was open for 17% of the time, Pallas kernels for 0%

commit v1 on v0

--- a/solution.py
+++ b/solution.py
@@ -17,8 +17,16 @@
 
 def apply_rows(matrix, right_side):
     return jnp.dot(
-        matrix, right_side, precision=lax.Precision.HIGHEST, preferred_element_type=jnp.float32
+        matrix, right_side, precision=lax.Precision.HIGH, preferred_element_type=jnp.float32
     )
+
+
+def mean_over_ctg(values, scenarios):
+    total = values
+    for step in range(1, scenarios):
+        pairs = [(i, (i + step) % scenarios) for i in range(scenarios)]
+        total = total + lax.ppermute(values, "ctg", pairs)
+    return total / scenarios
 
 
 def local(area_size, tie_peer, kkt_diag, kkt_offdiag, cost, consensus, dual, limit):
@@ -38,21 +46,19 @@
     linear = cost[0, 0]
     agreed = consensus[0, 0]
     dual_var = dual[0, 0]
+    spread = (dest[None, :] == jnp.arange(areas * pair_lines)[:, None]).astype(jnp.float32)
     for iteration in range(ITERS):
         right_side = live * (agreed - dual_var - linear)
         primal = live * (diagonal * right_side + apply_rows(offdiag, right_side))
-        primal_top = primal[:shared]
-        dual_top = dual_var[:shared]
-        shifted = primal_top + dual_top
-        gen_mean = lax.psum(shifted[:GENS], "ctg") / scenarios
-        empty = jnp.zeros((areas * pair_lines, hours), jnp.float32)
-        sent_primal = empty.at[dest].set(primal_top[GENS:])
-        sent_dual = empty.at[dest].set(dual_top[GENS:])
-        got_primal = lax.all_to_all(sent_primal, "area", split_axis=0, concat_axis=0, tiled=True)
-        got_dual = lax.all_to_all(sent_dual, "area", split_axis=0, concat_axis=0, tiled=True)
-        other = got_primal[dest] + got_dual[dest]
-        top_part = jnp.concatenate([gen_mean, 0.5 * (shifted[GENS:] + other)], axis=0)
-        averaged = jnp.concatenate([top_part, primal[shared:] + dual_var[shared:]], axis=0)
+        shifted = primal + dual_var
+        tie_part = shifted[GENS:shared]
+        sent = jnp.dot(spread, tie_part, precision=lax.Precision.HIGHEST)
+        got = lax.all_to_all(
+            sent.reshape(areas, pair_lines, hours), "area", split_axis=0, concat_axis=0, tiled=True
+        ).reshape(areas * pair_lines, hours)
+        gen_mean = mean_over_ctg(shifted[:GENS], scenarios)
+        other = jnp.dot(spread.T, got, precision=lax.Precision.HIGHEST)
+        averaged = jnp.concatenate([gen_mean, 0.5 * (tie_part + other), shifted[shared:]], axis=0)
         agreed = live * jnp.clip(averaged, -bound, bound)
         dual_var = live * (dual_var + primal - agreed)
     return (agreed[None, None], dual_var[None, None])

time: 140 us -> 69.2 us (0.49)
  waiting for transfers between devices: 33.6 us -> 12.6 us
  starting transfers between devices: 32.5 us -> 14.1 us
  other arithmetic: 19.3 us -> 4.32 us
  between operations: 14.6 us -> 1.64 us
  matrix products: 19.9 us -> 18.2 us
    all_to_all x6 -> x3, starting transfers between devices: 32.4 us -> 14 us  [local(): lax.all_to_all(sent.reshape(areas, pair_lines, hours), 'area', split_axis...]
    psum x3 -> x0, waiting for transfers between devices: 10.9 us -> none  [local(): gen_mean = lax.psum(shifted[:GENS], 'ctg') / scenarios]
    all_to_all x6 -> x3, waiting for transfers between devices: 22.6 us -> 12.6 us  [local(): lax.all_to_all(sent.reshape(areas, pair_lines, hours), 'area', split_axis...]
    unnamed x16 -> x18, local copies, waits for them, and re-layouts: 1 us -> 9.37 us
    all_to_all x12 -> x0, local copies, waits for them, and re-layouts: 5.53 us -> none  [the longest x6 2.77 us: local(): lax.all_to_all(sent_primal, 'area', split_axis=0, concat_axis=0, tiled=True)]
    add x6 -> x0, other arithmetic: 5.5 us -> none  [the longest x3 4.4 us: local(): primal[shared:] + dual_var[shared:]]
    mul x5 -> x0, other arithmetic: 5.27 us -> none  [the longest x2 4.41 us: local(): dual_var = live * (dual_var + primal - agreed)]
    scatter x6 -> x0, local copies, waits for them, and re-layouts: 5.22 us -> none  [the longest x3 2.75 us: local(): sent_primal = empty.at[dest].set(primal_top[GENS:])]
  transfers between devices with their start and end apart: 9 -> 6, of which waited for: 8 -> 3; matrix products, arithmetic and copies ran while one was open for 17% -> 14% of each run, Pallas kernels for 0% -> 0%
where the time goes in v1:
time: 69.2 us; the launch traced here: 68.6 us
  matrix products  18.2 us (26%)
  local copies, waits for them, and re-layouts  17.7 us (26%)
  starting transfers between devices  14.1 us (20%)
  waiting for transfers between devices  12.6 us (18%)
  other arithmetic  4.32 us (6%)
  between operations  1.64 us (2%)
    dot_general x3, matrix products, apply_rows(): jnp.dot(matrix, right_side, precision=lax.Precision.HIGH, preferred_eleme...  15.7 us
    all_to_all x3, starting transfers between devices, local(): lax.all_to_all(sent.reshape(areas, pair_lines, hours), 'area', split_axis...  14 us
    all_to_all x3, waiting for transfers between devices, local(): lax.all_to_all(sent.reshape(areas, pair_lines, hours), 'area', split_axis...  12.6 us
    unnamed x18, local copies, waits for them, and re-layouts  9.37 us
    slice x3, local copies, waits for them, and re-layouts, local(): shifted[shared:]  4.87 us
    reshape x3, local copies, waits for them, and re-layouts, local(): sent.reshape(areas, pair_lines, hours)  1.99 us
    dot_general x3, matrix products, local(): other = jnp.dot(spread.T, got, precision=lax.Precision.HIGHEST)  1.86 us
    broadcast_in_dim x1, other arithmetic, local(): return (agreed[None, None], dual_var[None, None])  1.48 us
  transfers between devices with their start and end apart: 6, of which 3 were waited for; matrix products, arithmetic and copies ran while one was open for 14% of the time, Pallas kernels for 0%

profile of v1, /device:TPU:0, one launch (start us, length us, event | category | flops | bytes accessed | tf_op | source)
XLA Modules:
  0.0 68.6 jit_solution(7661443100534675083)
XLA Ops:
  0.6 0.0 copy-start.4
  0.6 0.0 copy-start.5
  1.4 0.8 %convert_reduce_fusion = s32[42]{0:T(128)S(1)} fusion(s32[42]{0:T(128)} %bitcast.139), kind=kLoop, calls=%fused_computation.72 | loop fusion | flops 8778 | bytes 336 | tf_op jit(solution)/shard_map/reduce_sum | solution.py:14
  2.2 0.7 fusion.91
  2.9 1.6 %copy.40 = f32[1,1,1024,256]{2,3,1,0:T(8,128)S(1)} copy(f32[1,1,1024,256]{3,2,1,0:T(8,128)} %param.12) | data formatting | bytes 2097152 | tf_op args[4]
  4.4 1.6 %copy.38 = f32[1,1,1024,256]{2,3,1,0:T(8,128)S(1)} copy(f32[1,1,1024,256]{3,2,1,0:T(8,128)} %param.13) | data formatting | bytes 2097152 | tf_op args[5]
  6.0 0.0 copy-done.4
  6.0 1.3 %copy.39 = f32[1,1,1024,256]{2,3,1,0:T(8,128)} copy(f32[1,1,1024,256]{3,2,1,0:T(8,128)S(1)} %copy-done.4) | data formatting | bytes 2097152 | tf_op args[6]
  7.3 0.0 copy-done.5
  7.3 4.8 %fusion.39 = f32[1024,256]{0,1:T(8,128)S(1)} fusion(f32[1,1,1024,1024]{3,2,1,0:T(8,128)} %param.11, f32[1,1,1024,256]{2,3,1,0:T(8,128)S(1)} %copy.40, f32[1,1,1024,256]{2,3,1,0:T(8,128)} %copy.39, f32[1,1,1024,256]{2,3,1,0:T(8,128)S(1)} %copy.38, f32[1024]{0:T(1024)S(1)} %bitcast.136, f32[1024]{0:T(1024)S(1)} %fusion.90), kind=kOutput, calls=%fused_computation.17 | convolution fusion | flops 1613234176 | bytes 8396800 | tf_op jit(solution)/shard_map/dot_general | solution.py:19
  12.1 0.0 copy-start
  12.2 0.2 fusion.81
  12.4 0.7 %reshape.121 = f32[8,6,256]{2,1,0:T(8,128)} reshape(f32[48,256]{1,0:T(8,128)S(1)} %fusion.81) | data formatting | bytes 98304 | tf_op jit(solution)/shard_map/reshape | solution.py:57
  13.1 7.3 %all-to-all-start = ((f32[8,6,256]{2,1,0:T(8,128)}), f32[8,6,256]{2,1,0:T(8,128)S(1)}, u32[]{:S(2)}, u32[]{:S(2)}) async-start(f32[8,6,256]{2,1,0:T(8,128)} %reshape.121), calls=%async_computation | async-start | bytes 131072 | tf_op jit(solution)/shard_map/all_to_all | solution.py:56
  20.4 0.7 %slice.36 = f32[256,256]{0,1:T(8,128)} slice(f32[1024,256]{0,1:T(8,128)S(1)} %fusion.39), slice={[0:256], [0:256]} | slice | bytes 524288 | tf_op jit(solution)/shard_map/slice | solution.py:59
  21.1 0.0 collective-permute-start
  21.1 1.1 %slice.38 = f32[726,256]{0,1:T(8,128)} slice(f32[1024,256]{0,1:T(8,128)S(1)} %fusion.39), slice={[298:1024], [0:256]} | slice | bytes 1486848 | tf_op jit(solution)/shard_map/slice | solution.py:61
  22.3 1.6 %copy.36 = f32[1,1024,256]{1,2,0:T(8,128)S(1)} copy(f32[1,1024,256]{2,1,0:T(8,128)} %param.15) | data formatting | bytes 2097152 | tf_op args[7]
  23.8 3.5 %all-to-all-done = f32[8,6,256]{2,1,0:T(8,128)S(1)} async-done(((f32[8,6,256]{2,1,0:T(8,128)}), f32[8,6,256]{2,1,0:T(8,128)S(1)}, u32[]{:S(2)}, u32[]{:S(2)}) %all-to-all-start) | async-done | bytes 49184 | tf_op jit(solution)/shard_map/all_to_all | solution.py:56
  27.3 0.3 fusion.44
  27.6 0.0 collective-permute-done
  27.6 0.0 copy-done
  27.7 5.8 %fusion.36 = f32[1024,256]{0,1:T(8,128)S(1)} fusion(f32[1,1,1024,1024]{3,2,1,0:T(8,128)} %param.11, f32[1,1,1024,256]{2,3,1,0:T(8,128)S(1)} %copy.40, f32[1024,256]{0,1:T(8,128)} %copy-done, f32[726,256]{0,1:T(8,128)} %slice.38, f32[42,256]{0,1:T(8,128)S(1)} %fusion.44, f32[256,256]{0,1:T(8,128)S(1)} %add_multiply_fusion.2, f32[1,1024,256]{1,2,0:T(8,128)S(1)} %copy.36, ...), kind=kOutput, calls=%fused_computation.16 | convolution fusion | flops 1617428480 | bytes 9445376 | tf_op jit(solution)/shard_map/dot_general | solution.py:19
  33.5 0.2 fusion.79
  33.7 0.6 reshape.123
  34.4 3.3 %all-to-all-start.1 = ((f32[8,6,256]{2,1,0:T(8,128)}), f32[8,6,256]{2,1,0:T(8,128)S(1)}, u32[]{:S(2)}, u32[]{:S(2)}) async-start(f32[8,6,256]{2,1,0:T(8,128)} %reshape.123), calls=%async_computation.1 | async-start | bytes 131072 | tf_op jit(solution)/shard_map/all_to_all | solution.py:56
  37.7 0.7 %slice.39 = f32[256,256]{0,1:T(8,128)} slice(f32[1024,256]{0,1:T(8,128)S(1)} %fusion.36), slice={[0:256], [0:256]} | slice | bytes 524288 | tf_op jit(solution)/shard_map/slice | solution.py:59
  38.4 0.0 collective-permute-start.1
  38.4 1.1 %slice.41 = f32[726,256]{0,1:T(8,128)} slice(f32[1024,256]{0,1:T(8,128)S(1)} %fusion.36), slice={[298:1024], [0:256]} | slice | bytes 1486848 | tf_op jit(solution)/shard_map/slice | solution.py:61
  39.6 5.0 %all-to-all-done.1 = f32[8,6,256]{2,1,0:T(8,128)S(1)} async-done(((f32[8,6,256]{2,1,0:T(8,128)}), f32[8,6,256]{2,1,0:T(8,128)S(1)}, u32[]{:S(2)}, u32[]{:S(2)}) %all-to-all-start.1) | async-done | bytes 49184 | tf_op jit(solution)/shard_map/all_to_all | solution.py:56
  44.6 0.3 fusion.43
  44.9 0.0 collective-permute-done.1
  44.9 5.1 %fusion.33 = f32[1024,256]{0,1:T(8,128)S(1)} fusion(f32[1,1,1024,1024]{3,2,1,0:T(8,128)} %param.11, f32[1,1,1024,256]{2,3,1,0:T(8,128)S(1)} %copy.40, f32[1024,256]{0,1:T(8,128)S(1)} %fusion.36, f32[726,256]{0,1:T(8,128)} %slice.41, f32[42,256]{0,1:T(8,128)S(1)} %fusion.43, f32[256,256]{0,1:T(8,128)S(1)} %add_multiply_fusion.1, ...), kind=kOutput, calls=%fused_computation.15 | convolution fusion | flops 1617428480 | bytes 9445376 | tf_op jit(solution)/shard_map/dot_general | solution.py:19
  50.0 0.0 copy-start.1
  50.0 0.2 fusion.77
  50.2 0.8 %copy-done.1 = f32[1024,256]{0,1:T(8,128)} copy-done((f32[1024,256]{0,1:T(8,128)}, f32[1024,256]{0,1:T(8,128)S(1)}, u32[]{:S(2)}) %copy-start.1) | copy-done | bytes 1048600
  51.0 0.0 copy-start.2
  51.0 0.6 reshape.125
  51.6 3.3 %all-to-all-start.2 = ((f32[8,6,256]{2,1,0:T(8,128)}), f32[8,6,256]{2,1,0:T(8,128)S(1)}, u32[]{:S(2)}, u32[]{:S(2)}) async-start(f32[8,6,256]{2,1,0:T(8,128)} %reshape.125), calls=%async_computation.2 | async-start | bytes 131072 | tf_op jit(solution)/shard_map/all_to_all | solution.py:56
  55.0 0.1 collective-permute-start.2
  55.1 2.6 %fusion.94 = (f32[726,256]{0,1:T(8,128)}, f32[1,1,726,256]{2,3,1,0:T(8,128)}) fusion(f32[1024,256]{0,1:T(8,128)} %copy-done.1), kind=kLoop, calls=%fused_computation.88 | loop fusion | bytes 2230272 | tf_op jit(solution)/shard_map/slice | solution.py:61
  57.6 4.2 %all-to-all-done.2 = f32[8,6,256]{2,1,0:T(8,128)S(1)} async-done(((f32[8,6,256]{2,1,0:T(8,128)}), f32[8,6,256]{2,1,0:T(8,128)S(1)}, u32[]{:S(2)}, u32[]{:S(2)}) %all-to-all-start.2) | async-done | bytes 49184 | tf_op jit(solution)/shard_map/all_to_all | solution.py:56
  61.8 0.0 copy-start.3
  61.9 1.3 %fusion.42 = f32[42,256]{0,1:T(8,128)S(1)} fusion(f32[48,256]{1,0:T(8,128)S(1)} %reshape.126, f32[1024,256]{0,1:T(8,128)} %copy-done.1, s32[42]{0:T(128)S(1)} %fusion.91), kind=kOutput, calls=%fused_computation.19 | convolution fusion | flops 6216672 | bytes 135336 | tf_op jit(solution)/shard_map/dot_general | solution.py:60
  63.1 0.0 collective-permute-done.2
  63.1 1.0 %add_multiply_fusion = f32[256,256]{0,1:T(8,128)S(1)} fusion(f32[256,256]{0,1:T(8,128)S(1)} %collective-permute-done.2, f32[1024,256]{0,1:T(8,128)} %copy-done.1), kind=kLoop, calls=%fused_computation.62 | loop fusion | flops 131072 | bytes 786432 | tf_op jit(solution)/shard_map/div | solution.py:29
  64.1 0.0 copy-done.2
  64.1 1.5 %fusion.55 = f32[1,1,1024,256]{2,3,1,0:T(8,128)S(1)} fusion(f32[1024,256]{0,1:T(8,128)S(1)} %copy-done.2, f32[726,256]{0,1:T(8,128)} %get-tuple-element.8, f32[42,256]{0,1:T(8,128)S(1)} %fusion.42, f32[256,256]{0,1:T(8,128)S(1)} %add_multiply_fusion, f32[1,1024,256]{1,2,0:T(8,128)S(1)} %copy.36, f32[1024]{0:T(1024)S(1)} %fusion.90), kind=kLoop, calls=%fused_computation.38 | loop fusion | flops 2097152 | bytes 4198400 | tf_op jit(solution)/shard_map/broadcast_in_dim | solution.py:64
  65.6 0.0 copy-done.3
  65.6 0.3 fusion.50
  65.9 1.3 %copy.47 = f32[1,1,1024,256]{3,2,1,0:T(8,128)} copy(f32[1,1,1024,256]{2,3,1,0:T(8,128)S(1)} %fusion.50) | data formatting | bytes 2097152
  67.2 1.3 %copy.48 = f32[1,1,1024,256]{3,2,1,0:T(8,128)} copy(f32[1,1,1024,256]{2,3,1,0:T(8,128)S(1)} %fusion.55) | data formatting | bytes 2097152
  (7 shorter events, 0.1 us)
Async XLA Ops:
  0.6 5.4 %copy-start.4 = (f32[1,1,1024,256]{3,2,1,0:T(8,128)S(1)}, f32[1,1,1024,256]{3,2,1,0:T(8,128)}, u32[]{:S(2)}) copy-start(f32[1,1,1024,256]{3,2,1,0:T(8,128)} %param.14) | copy-start | bytes 3145732
  0.6 6.7 %copy-start.5 = (f32[1,1,1024]{2,1,0:T(1,128)S(1)}, f32[1,1,1024]{2,1,0:T(1,128)}, u32[]{:S(2)}) copy-start(f32[1,1,1024]{2,1,0:T(1,128)} %param.10) | copy-start | bytes 12292
  12.1 15.5 %copy-start = (f32[1024,256]{0,1:T(8,128)}, f32[1024,256]{0,1:T(8,128)S(1)}, u32[]{:S(2)}) copy-start(f32[1024,256]{0,1:T(8,128)S(1)} %fusion.39) | copy-start | bytes 3145732
  13.1 14.2 %all-to-all-start = ((f32[8,6,256]{2,1,0:T(8,128)}), f32[8,6,256]{2,1,0:T(8,128)S(1)}, u32[]{:S(2)}, u32[]{:S(2)}) async-start(f32[8,6,256]{2,1,0:T(8,128)} %reshape.121), calls=%async_computation | async-start | bytes 131072 | tf_op jit(solution)/shard_map/all_to_all | solution.py:56
  21.1 6.5 %collective-permute-start = (f32[256,256]{0,1:T(8,128)}, f32[256,256]{0,1:T(8,128)S(1)}, u32[]{:S(2)}, u32[]{:S(2)}) collective-permute-start(f32[256,256]{0,1:T(8,128)} %slice.36), channel_id=1, source_target_pairs={{0,1},{1,0},{2,3},{3,2},{4,5},{5,4},{6,7},{7,6},{8,9},{9,8},{10,11... | collective-permute-start | bytes 786440 | tf_op jit(solution)/shard_map/ppermute | solution.py:28
  34.4 10.2 %all-to-all-start.1 = ((f32[8,6,256]{2,1,0:T(8,128)}), f32[8,6,256]{2,1,0:T(8,128)S(1)}, u32[]{:S(2)}, u32[]{:S(2)}) async-start(f32[8,6,256]{2,1,0:T(8,128)} %reshape.123), calls=%async_computation.1 | async-start | bytes 131072 | tf_op jit(solution)/shard_map/all_to_all | solution.py:56
  38.4 6.4 %collective-permute-start.1 = (f32[256,256]{0,1:T(8,128)}, f32[256,256]{0,1:T(8,128)S(1)}, u32[]{:S(2)}, u32[]{:S(2)}) collective-permute-start(f32[256,256]{0,1:T(8,128)} %slice.39), channel_id=1, source_target_pairs={{0,1},{1,0},{2,3},{3,2},{4,5},{5,4},{6,7},{7,6},{8,9},{9,8},{10,11... | collective-permute-start | bytes 786440 | tf_op jit(solution)/shard_map/ppermute | solution.py:28
  50.0 1.0 %copy-start.1 = (f32[1024,256]{0,1:T(8,128)}, f32[1024,256]{0,1:T(8,128)S(1)}, u32[]{:S(2)}) copy-start(f32[1024,256]{0,1:T(8,128)S(1)} %fusion.33) | copy-start | bytes 3145732
  51.0 13.1 %copy-start.2 = (f32[1024,256]{0,1:T(8,128)S(1)}, f32[1024,256]{0,1:T(8,128)}, u32[]{:S(2)}) copy-start(f32[1024,256]{0,1:T(8,128)} %copy-done.1) | copy-start | bytes 3145732
  51.6 10.2 %all-to-all-start.2 = ((f32[8,6,256]{2,1,0:T(8,128)}), f32[8,6,256]{2,1,0:T(8,128)S(1)}, u32[]{:S(2)}, u32[]{:S(2)}) async-start(f32[8,6,256]{2,1,0:T(8,128)} %reshape.125), calls=%async_computation.2 | async-start | bytes 131072 | tf_op jit(solution)/shard_map/all_to_all | solution.py:56
  55.0 8.1 %collective-permute-start.2 = (f32[256,256]{0,1:T(8,128)S(1)}, f32[256,256]{0,1:T(8,128)S(1)}, u32[]{:S(2)}, u32[]{:S(2)}) collective-permute-start(f32[256,256]{0,1:T(8,128)S(1)} %slice.42), channel_id=1, source_target_pairs={{0,1},{1,0},{2,3},{3,2},{4,5},{5,4},{6,7},{7,6},{8,9},{9,8},{10,11... | collective-permute-start | bytes 786440 | tf_op jit(solution)/shard_map/ppermute | solution.py:28
  61.8 3.8 %copy-start.3 = (f32[1,1,726,256]{2,3,1,0:T(8,128)S(1)}, f32[1,1,726,256]{2,3,1,0:T(8,128)}, u32[]{:S(2)}) copy-start(f32[1,1,726,256]{2,3,1,0:T(8,128)} %get-tuple-element.9) | copy-start | bytes 2230276
